TPU v7x, 256 devices: a whole 4x4x8 slice. The times are simulated.
256 devices in a mesh: req: 32 (over z, x), tp: 8 (over y, core).
Axes of the slice: x: 4, y: 4, z: 8, core: 2. Of those that a mesh axis runs over, the one named last changes fastest.
Arguments:
- hidden_in: bfloat16 [32768, 2048], P('req'), may hold values from -6 to 6
- qkv_weight: bfloat16 [2048, 3, 2048], P(None, None, 'tp'), may hold values from -0.125 to 0.125
- out_weight: bfloat16 [2048, 2048], P('tp'), may hold values from -1.5 to 1.5
- kv_pool: bfloat16 [512, 2, 128, 2048], P('req', None, None, 'tp'), may hold values from -48 to 48
- cached_len: int32 [32], replicated, may hold values from 3585 to 4096, as said below
- page_slot: int32 [32, 32], replicated, may hold values from 0 to 15
- page_holder: int32 [32, 32, 1], replicated, may hold values from 0 to 31; in each aligned block of 32 rows (0 to 31, 32 to 63, ..., all dimensions but the last counted through in order) at most 2 rows name the same one
- cont_flag: int32 [32], replicated, may hold values 0 or 1
Outputs:
- attn_out: bfloat16 [32768, 2048], P(('req', 'tp'))
Inputs may be any that keep to these rules, and one draw needn't show every extreme that they name: `page_holder`: within the table entries of the requests of one index of req (aligned blocks of 1 request), no holder is named more than 2 times. `cached_len`: A cached length of 4096 occurs in every draw. `page_slot`: page slot k of holder h is row h * 16 + k of kv_pool.
All inputs are finite; a program needn't handle non-finite values.
Results may differ from a plain program's by a relative error of at most 0.02.
Values may be sent and summed in bfloat16 or wider, within the bound.
A program may use at most 128 MiB of HBM per device.

v0:
```python
import jax
import jax.numpy as jnp
from jax import lax
from jax.sharding import PartitionSpec as P

HD = 128
NEW = 1024
PAGE = 128
MAXP = 32


def rotate(feature, position):
    half_width = feature.shape[-1] // 2
    indices = jnp.arange(half_width).astype(jnp.float32)
    inverse = jnp.exp(indices * (-2.0 / feature.shape[-1]) * jnp.log(jnp.float32(10000.0)))
    angles = position[:, None, None] * inverse[None, None, :]
    cosine = jnp.cos(angles)
    sine_part = jnp.sin(angles)
    first_half = feature[..., :half_width]
    second_half = feature[..., half_width:]
    return jnp.concatenate(
        [
            first_half * cosine - second_half * sine_part,
            second_half * cosine + first_half * sine_part,
        ],
        axis=-1,
    )


def attend_block(query_part, keys_part, values_part, allowed):
    scores = jnp.einsum(
        "qd,kd->qk", query_part, keys_part, preferred_element_type=jnp.float32
    ) * HD ** (-0.5)
    scores = jnp.where(allowed, scores, -1e30)
    row_top = jnp.max(scores, axis=-1)
    weights = jnp.where(allowed, jnp.exp(scores - row_top[:, None]), 0.0)
    row_total = jnp.sum(weights, axis=-1)
    summed = jnp.einsum(
        "qk,kd->qd", weights.astype(jnp.bfloat16), values_part, preferred_element_type=jnp.float32
    )
    return (summed, row_top, row_total)


def body(hidden_in, qkv_weight, out_weight, kv_pool, cached_len, page_slot, page_holder, cont_flag):
    req_count = lax.axis_size("req")
    tp_count = lax.axis_size("tp")
    req_index = lax.axis_index("req")
    local_reqs = hidden_in.shape[0] // NEW
    local_width = qkv_weight.shape[2]
    local_heads = local_width // HD
    table_block = local_reqs * MAXP
    capacity = max(2, 2 * table_block // req_count)
    cache_span = MAXP * PAGE
    holder_rows = page_holder[:, :, 0]
    held_here = holder_rows == req_index
    ranking = jnp.cumsum(held_here.astype(jnp.int32), axis=1) - 1
    picked = held_here[:, :, None] & (ranking[:, :, None] == jnp.arange(capacity)[None, None, :])
    send_slots = jnp.sum(jnp.where(picked, page_slot[:, :, None], 0), axis=1)
    outgoing = kv_pool[send_slots]
    lengths = lax.dynamic_slice_in_dim(cached_len, req_index * local_reqs, local_reqs)
    flags = lax.dynamic_slice_in_dim(cont_flag, req_index * local_reqs, local_reqs)
    live_len = lengths * flags
    token_rows = hidden_in.astype(jnp.float32)
    centre = jnp.mean(token_rows, axis=-1, keepdims=True)
    centred = token_rows - centre
    spread = jnp.mean(centred * centred, axis=-1, keepdims=True)
    normed = (centred * lax.rsqrt(spread + 1e-05)).astype(jnp.bfloat16)
    united_qkv = jnp.einsum("td,dcf->tcf", normed, qkv_weight, preferred_element_type=jnp.float32)
    positions = (live_len[:, None] + jnp.arange(NEW)[None, :]).astype(jnp.float32).reshape(-1)
    query_rot = rotate(united_qkv[:, 0].reshape(-1, local_heads, HD), positions).astype(
        jnp.bfloat16
    )
    new_key = rotate(united_qkv[:, 1].reshape(-1, local_heads, HD), positions).astype(jnp.bfloat16)
    new_value = united_qkv[:, 2].reshape(-1, local_heads, HD).astype(jnp.bfloat16)
    row_count = local_reqs * NEW
    block_rows = min(512, NEW)
    req_blocks = NEW // block_rows
    row_blocks = row_count // block_rows
    work_items = local_heads * row_blocks
    query_heads = query_rot.transpose(1, 0, 2)
    new_places = jnp.arange(NEW)[None, :]

    def block_place(index):
        head = index // row_blocks
        block = index % row_blocks
        owner = block // req_blocks
        query_pos = block % req_blocks * block_rows + jnp.arange(block_rows)
        query_part = lax.dynamic_slice(
            query_heads, (head, block * block_rows, 0), (1, block_rows, HD)
        )[0]
        return (head, owner, query_pos, query_part)

    incoming = lax.all_to_all(outgoing, "req", split_axis=0, concat_axis=0, tiled=True)
    own_holders = lax.dynamic_index_in_dim(holder_rows, req_index, 0, keepdims=False)
    same_holder = own_holders[:, None] == own_holders[None, :]
    earlier = jnp.arange(table_block)[None, :] < jnp.arange(table_block)[:, None]
    own_rank = jnp.sum((same_holder & earlier).astype(jnp.int32), axis=1)
    fetched = incoming.reshape(req_count * capacity, 2, PAGE, local_width)[
        own_holders * capacity + own_rank
    ]
    fetched = fetched.reshape(local_reqs, MAXP, 2, PAGE, local_width)
    cache_key = fetched[:, :, 0].reshape(local_reqs, cache_span, local_heads, HD)
    cache_value = fetched[:, :, 1].reshape(local_reqs, cache_span, local_heads, HD)
    keys_all = jnp.concatenate(
        [cache_key, new_key.reshape(local_reqs, NEW, local_heads, HD)], axis=1
    )
    values_all = jnp.concatenate(
        [cache_value, new_value.reshape(local_reqs, NEW, local_heads, HD)], axis=1
    )

    def joined_block(index):
        head, owner, query_pos, query_part = block_place(index)
        keys_part = lax.dynamic_slice(
            keys_all, (owner, 0, head, 0), (1, cache_span + NEW, 1, HD)
        ).reshape(cache_span + NEW, HD)
        values_part = lax.dynamic_slice(
            values_all, (owner, 0, head, 0), (1, cache_span + NEW, 1, HD)
        ).reshape(cache_span + NEW, HD)
        live_one = lax.dynamic_index_in_dim(live_len, owner, 0, keepdims=False)
        cache_ok = jnp.broadcast_to(
            jnp.arange(cache_span)[None, :] < live_one, (block_rows, cache_span)
        )
        allowed = jnp.concatenate([cache_ok, new_places <= query_pos[:, None]], axis=1)
        summed, row_top, row_total = attend_block(query_part, keys_part, values_part, allowed)
        return (summed / row_total[:, None]).astype(jnp.bfloat16)

    blocks_out = lax.map(joined_block, jnp.arange(work_items))
    attended = (
        blocks_out.reshape(local_heads, row_count, HD)
        .transpose(1, 0, 2)
        .reshape(row_count, local_width)
    )
    share_rows = row_count // tp_count
    head_term = jnp.dot(attended, out_weight, preferred_element_type=jnp.float32)
    summed_rows = lax.psum(head_term.astype(jnp.bfloat16), "tp")
    result = lax.dynamic_slice_in_dim(summed_rows, lax.axis_index("tp") * share_rows, share_rows, 0)
    return result


def solution(mesh):
    in_specs = (
        P("req", None),
        P(None, None, "tp"),
        P("tp", None),
        P("req", None, None, "tp"),
        P(),
        P(),
        P(),
        P(),
    )
    out_specs = P(("req", "tp"), None)
    return jax.shard_map(body, mesh=mesh, in_specs=in_specs, out_specs=out_specs, check_vma=False)
```

profile of v0, /device:TPU:2, one launch (start us, length us, event | category | flops | bytes accessed | tf_op | source)
XLA Modules:
  0.0 384.3 jit_solution(15847027432307803292)
XLA Ops:
  6.5 0.9 broadcast_compare_fusion
  7.6 0.8 select_reduce_fusion
  8.7 7.0 %gather_fusion = bf16[64,2,128,256]{3,2,1,0:T(8,128)(2,1)} fusion(bf16[16,2,128,256]{3,2,1,0:T(8,128)(2,1)} %param.13, s32[1024]{0:T(1024)S(1)} %pad_clamp_fusion.1), kind=kCustom, calls=%fused_computation | custom fusion | bytes 16777472 | tf_op jit(solution)/shard_map/gather | solution.py:59
  15.7 11.8 %all-to-all-start = ((bf16[32,2,2,128,256]{4,3,2,1,0:T(8,128)(2,1)}), bf16[32,2,2,128,256]{4,3,2,1,0:T(8,128)(2,1)}, u32[]{:S(2)}, u32[]{:S(2)}) async-start(bf16[32,2,2,128,256]{4,3,2,1,0:T(8,128)(2,1)} %bitcast.83), calls=%async_computation | async-start | bytes 16777216 | tf_op jit(solution)/shard_map/all_to_all | solution.py:93
  27.6 0.7 dynamic_slice.43
  28.9 2.8 convert_reduce_fusion
  31.7 1.2 fusion.39
  32.9 4.0 %fusion.42 = f32[1024,3,256]{0,2,1:T(8,128)S(1)} fusion(bf16[2048,3,256]{2,0,1:T(8,128)(2,1)S(1)} %copy-done, bf16[1024,2048]{1,0:T(8,128)(2,1)S(1)} %copy-done.2, f32[1024]{0:T(1024)S(1)} %add_rsqrt_fusion, f32[1024]{0:T(1024)S(1)} %broadcast_multiply_fusion), kind=kOutput, calls=%fused_computation.34 | convolution fusion | flops 3229614080 | bytes 10493952 | tf_op jit(solution)/shard_map/td,dcf->tcf/dot_general | solution.py:68
  37.0 1.6 copy-done.5
  38.7 1.0 copy.44
  39.7 1.8 fusion.55
  41.5 0.9 fusion.56
  42.8 0.9 fusion.57
  44.0 1.4 copy.50
  45.4 2.4 copy.48
  49.9 0.7 fusion.50
  50.6 1.9 multiply_cosine_fusion
  52.5 2.8 fusion.46
  55.3 1.1 maximum_bitcast_fusion
  56.4 160.8 %all-to-all-done = bf16[32,2,2,128,256]{4,3,2,1,0:T(8,128)(2,1)} async-done(((bf16[32,2,2,128,256]{4,3,2,1,0:T(8,128)(2,1)}), bf16[32,2,2,128,256]{4,3,2,1,0:T(8,128)(2,1)}, u32[]{:S(2)}, u32[]{:S(2)}) %all-to-all-start) | async-done | bytes 8388640 | tf_op jit(solution)/shard_map/all_to_all | solution.py:93
  217.2 6.1 %gather_fusion.1 = bf16[32,2,128,256]{3,2,1,0:T(8,128)(2,1)} fusion(bf16[64,2,128,256]{3,2,1,0:T(8,128)(2,1)} %bitcast.6, s32[1024]{0:T(1024)S(1)} %pad_clamp_fusion), kind=kCustom, calls=%fused_computation.1 | custom fusion | bytes 8388736 | tf_op jit(solution)/shard_map/gather | solution.py:98
  223.4 4.7 %fusion.54 = (bf16[1,32,1,128,256]{4,3,2,1,0:T(8,128)(2,1)}, bf16[1,32,1,128,256]{4,3,2,1,0:T(8,128)(2,1)}) fusion(bf16[1,32,2,128,256]{4,3,2,1,0:T(8,128)(2,1)} %bitcast.84), kind=kLoop, calls=%fused_computation.74 | loop fusion | bytes 8388608 | tf_op jit(solution)/shard_map/slice | solution.py:103
  228.0 2.5 reshape_squeeze.16
  230.6 1.6 copy.43
  232.2 2.5 reshape_squeeze.14
  235.1 1.3 copy-done.3
  236.7 2.3 maximum_maximum_fusion
  239.0 46.8 %while.13 = (s32[]{:T(128)}, bf16[4,512,128]{2,1,0:T(8,128)(2,1)}, s32[1]{0:T(128)}, s32[4]{0:T(128)S(1)}, bf16[2,1024,128]{2,1,0:T(8,128)(2,1)}, /*index=5*/bf1...) while((s32[]{:T(128)}, bf16[4,512,128]{2,1,0:T(8,128)(2,1)}, ...), condition=%wide.region_8.9_spmd.clone, body=%wide.region_5.8_spmd.clone.sunk | while | flops 1374293504 | bytes 46968904 | solution.py:127
  239.0 0.7 dynamic_slice.87
  242.9 2.9 fusion.68
  245.8 2.5 fusion.69
  248.3 2.4 fusion.70
  250.7 0.7 dynamic_slice.87
  254.6 2.9 fusion.68
  257.5 2.5 fusion.69
  260.0 2.4 fusion.70
  262.4 0.7 dynamic_slice.87
  266.3 2.9 fusion.68
  269.2 2.5 fusion.69
  271.7 2.4 fusion.70
  274.1 0.7 dynamic_slice.87
  278.0 2.9 fusion.68
  280.9 2.5 fusion.69
  283.4 2.4 fusion.70
  285.8 2.0 copy.45
  287.8 4.8 %convolution_convert_fusion = bf16[1024,2048]{1,0:T(8,128)(2,1)} fusion(bf16[1024,256]{0,1:T(8,128)(2,1)} %bitcast.87, bf16[256,2048]{1,0:T(8,128)(2,1)} %param.12), kind=kOutput, calls=%fused_computation.37 | convolution fusion | flops 1075838976 | bytes 5767168 | tf_op jit(solution)/shard_map/dot_general | solution.py:134
  292.6 83.0 %all-reduce.2.cloned.1.call-done = bf16[1024,2048]{1,0:T(8,128)(2,1)} async-done(((bf16[1024,2048]{1,0:T(8,128)(2,1)}), bf16[1024,2048]{1,0:T(8,128)(2,1)}) %all-reduce.2.cloned.1.call-update) | async-done | bytes 4194320 | tf_op jit(solution)/shard_map/psum | solution.py:135
  375.6 1.9 constant_dynamic-slice_fusion.1
  (65 shorter events, 4.9 us)
Async XLA Ops:
  6.5 26.4 %copy-start = (bf16[2048,3,256]{2,0,1:T(8,128)(2,1)S(1)}, bf16[2048,3,256]{2,0,1:T(8,128)(2,1)}, u32[]{:S(2)}) copy-start(bf16[2048,3,256]{2,0,1:T(8,128)(2,1)} %param.11) | copy-start | bytes 9437188
  15.7 11.9 %copy-start.9 = (s32[32]{0:T(128)S(1)}, s32[32]{0:T(128)}, u32[]{:S(2)}) copy-start(s32[32]{0:T(128)} %param.17) | copy-start | bytes 388
  15.7 12.6 %copy-start.10 = (s32[32]{0:T(128)S(1)}, s32[32]{0:T(128)}, u32[]{:S(2)}) copy-start(s32[32]{0:T(128)} %param.14) | copy-start | bytes 388
  15.7 201.5 %all-to-all-start = ((bf16[32,2,2,128,256]{4,3,2,1,0:T(8,128)(2,1)}), bf16[32,2,2,128,256]{4,3,2,1,0:T(8,128)(2,1)}, u32[]{:S(2)}, u32[]{:S(2)}) async-start(bf16[32,2,2,128,256]{4,3,2,1,0:T(8,128)(2,1)} %bitcast.83), calls=%async_computation | async-start | bytes 16777216 | tf_op jit(solution)/shard_map/all_to_all | solution.py:93
  27.5 348.1 %all-reduce.2.cloned.1.call-start = ((), (), s32[]{:S(2)}) async-start(), calls=%async_computation.1 | async-start | bytes 8388608 | tf_op jit(solution)/shard_map/psum | solution.py:135
  27.5 4.1 %copy-start.2 = (bf16[1024,2048]{1,0:T(8,128)(2,1)S(1)}, bf16[1024,2048]{1,0:T(8,128)(2,1)}, u32[]{:S(2)}) copy-start(bf16[1024,2048]{1,0:T(8,128)(2,1)} %param.10) | copy-start | bytes 12582916
  37.0 1.7 copy-start.5
  234.7 1.6 copy-start.3
  234.7 1.7 copy-start.6
  234.8 1.8 copy-start.7
  234.8 2.0 copy-start.8
  245.8 2.5 copy-start.4
  257.5 2.5 copy-start.4
  269.2 2.5 copy-start.4
  280.9 2.5 copy-start.4
  287.8 89.6 %copy-start.1 = (bf16[2048,3,256]{2,0,1:T(8,128)(2,1)S(1)}, bf16[2048,3,256]{2,0,1:T(8,128)(2,1)}, u32[]{:S(2)}) copy-start(bf16[2048,3,256]{2,0,1:T(8,128)(2,1)} %param.11) | copy-start | bytes 9437188
Sparse Core Ops, SparseCore 0:
  292.7 82.8 all-reduce.1
where the time goes:
time: 385 us; the launch traced here: 384 us
  waiting for transfers between devices  244 us (63%)
  local copies, waits for them, and re-layouts  46 us (12%)
  matrix products  30 us (8%)
  other arithmetic  26.4 us (7%)
  between operations  14.9 us (4%)
  starting transfers between devices  11.8 us (3%)
  loops' own time  11.4 us (3%)
    all_to_all x1, waiting for transfers between devices, body(): lax.all_to_all(outgoing, 'req', split_axis=0, concat_axis=0, tiled=True)  161 us
    psum x1, waiting for transfers between devices, body(): summed_rows = lax.psum(head_term.astype(jnp.bfloat16), 'tp')  83 us
    all_to_all x1, starting transfers between devices, body(): lax.all_to_all(outgoing, 'req', split_axis=0, concat_axis=0, tiled=True)  11.8 us
    dot_general x4, matrix products, attend_block(): jnp.einsum('qd,kd->qk', query_part, keys_part, preferred_element_type=jnp...  11.5 us
    another operation x1, loops' own time, body(): blocks_out = lax.map(joined_block, jnp.arange(work_items))  11.4 us
    reduce_sum x4, other arithmetic, attend_block(): row_total = jnp.sum(weights, axis=-1)  9.99 us
    dot_general x4, matrix products, attend_block(): jnp.einsum('qk,kd->qd', weights.astype(jnp.bfloat16), values_part, prefer...  9.69 us
    unnamed x24, local copies, waits for them, and re-layouts  7.73 us
  transfers between devices with their start and end apart: 2, of which 2 were waited for; matrix products, arithmetic and copies ran while one was open for 7% of the time, Pallas kernels for 0%

commit v1 on v0

--- a/solution.py
+++ b/solution.py
@@ -132,7 +132,9 @@
     )
     share_rows = row_count // tp_count
     head_term = jnp.dot(attended, out_weight, preferred_element_type=jnp.float32)
-    summed_rows = lax.psum(head_term.astype(jnp.bfloat16), "tp")
+    own = head_term.astype(jnp.bfloat16)
+    blocks = lax.all_gather(own, "tp")
+    summed_rows = jnp.sum(blocks, axis=0)
     result = lax.dynamic_slice_in_dim(summed_rows, lax.axis_index("tp") * share_rows, share_rows, 0)
     return result
 

time: 385 us -> 481 us (1.25)
  waiting for transfers between devices: 244 us -> 325 us
  other arithmetic: 26.4 us -> 40.9 us
    all_gather x0 -> x1, waiting for transfers between devices: none -> 164 us  [body(): blocks = lax.all_gather(own, 'tp')]
    psum x1 -> x0, waiting for transfers between devices: 83 us -> none  [body(): summed_rows = lax.psum(head_term.astype(jnp.bfloat16), 'tp')]
    reduce_sum x0 -> x1, other arithmetic: none -> 14.5 us  [body(): summed_rows = jnp.sum(blocks, axis=0)]
  transfers between devices with their start and end apart: 2 -> 2, of which waited for: 2 -> 2; matrix products, arithmetic and copies ran while one was open for 7% -> 5% of each run, Pallas kernels for 0% -> 0%
where the time goes in v1:
time: 481 us; the launch traced here: 479 us
  waiting for transfers between devices  325 us (68%)
  local copies, waits for them, and re-layouts  45.2 us (9%)
  other arithmetic  40.9 us (9%)
  matrix products  29.8 us (6%)
  between operations  14.9 us (3%)
  starting transfers between devices  11.8 us (2%)
  loops' own time  11.4 us (2%)
    all_gather x1, waiting for transfers between devices, body(): blocks = lax.all_gather(own, 'tp')  164 us
    all_to_all x1, waiting for transfers between devices, body(): lax.all_to_all(outgoing, 'req', split_axis=0, concat_axis=0, tiled=True)  161 us
    reduce_sum x1, other arithmetic, body(): summed_rows = jnp.sum(blocks, axis=0)  14.5 us
    all_to_all x1, starting transfers between devices, body(): lax.all_to_all(outgoing, 'req', split_axis=0, concat_axis=0, tiled=True)  11.8 us
    dot_general x4, matrix products, attend_block(): jnp.einsum('qd,kd->qk', query_part, keys_part, preferred_element_type=jnp...  11.5 us
    another operation x1, loops' own time, body(): blocks_out = lax.map(joined_block, jnp.arange(work_items))  11.4 us
    reduce_sum x4, other arithmetic, attend_block(): row_total = jnp.sum(weights, axis=-1)  9.99 us
    dot_general x4, matrix products, attend_block(): jnp.einsum('qk,kd->qd', weights.astype(jnp.bfloat16), values_part, prefer...  9.69 us
  transfers between devices with their start and end apart: 2, of which 2 were waited for; matrix products, arithmetic and copies ran while one was open for 5% of the time, Pallas kernels for 0%

profile of v1, /device:TPU:2, one launch (start us, length us, event | category | flops | bytes accessed | tf_op | source)
XLA Modules:
  0.0 478.7 jit_solution(9160877212912081910)
XLA Ops:
  6.5 0.9 broadcast_compare_fusion
  7.6 0.8 select_reduce_fusion
  8.7 7.0 %gather_fusion = bf16[64,2,128,256]{3,2,1,0:T(8,128)(2,1)} fusion(bf16[16,2,128,256]{3,2,1,0:T(8,128)(2,1)} %param.13, s32[1024]{0:T(1024)S(1)} %pad_clamp_fusion.1), kind=kCustom, calls=%fused_computation | custom fusion | bytes 16777472 | tf_op jit(solution)/shard_map/gather | solution.py:59
  15.7 11.8 %all-to-all-start = ((bf16[32,2,2,128,256]{4,3,2,1,0:T(8,128)(2,1)}), bf16[32,2,2,128,256]{4,3,2,1,0:T(8,128)(2,1)}, u32[]{:S(2)}, u32[]{:S(2)}) async-start(bf16[32,2,2,128,256]{4,3,2,1,0:T(8,128)(2,1)} %bitcast.85), calls=%async_computation | async-start | bytes 16777216 | tf_op jit(solution)/shard_map/all_to_all | solution.py:93
  27.6 0.7 dynamic_slice.43
  28.9 2.8 convert_reduce_fusion
  31.7 1.2 fusion.39
  32.9 4.0 fusion.42
  37.0 1.6 copy-done.5
  38.7 1.0 copy.44
  39.7 1.8 fusion.55
  41.5 0.9 fusion.56
  42.8 0.9 fusion.57
  44.0 1.4 copy.50
  45.4 2.4 copy.48
  49.9 0.7 fusion.50
  50.6 1.9 multiply_cosine_fusion
  52.5 2.8 fusion.46
  55.3 1.1 maximum_bitcast_fusion
  56.4 160.8 %all-to-all-done = bf16[32,2,2,128,256]{4,3,2,1,0:T(8,128)(2,1)} async-done(((bf16[32,2,2,128,256]{4,3,2,1,0:T(8,128)(2,1)}), bf16[32,2,2,128,256]{4,3,2,1,0:T(8,128)(2,1)}, u32[]{:S(2)}, u32[]{:S(2)}) %all-to-all-start) | async-done | bytes 8388640 | tf_op jit(solution)/shard_map/all_to_all | solution.py:93
  217.2 6.1 %gather_fusion.1 = bf16[32,2,128,256]{3,2,1,0:T(8,128)(2,1)} fusion(bf16[64,2,128,256]{3,2,1,0:T(8,128)(2,1)} %bitcast.6, s32[1024]{0:T(1024)S(1)} %pad_clamp_fusion), kind=kCustom, calls=%fused_computation.1 | custom fusion | bytes 8388736 | tf_op jit(solution)/shard_map/gather | solution.py:98
  223.4 4.7 fusion.54
  228.0 2.5 reshape_squeeze.16
  230.6 1.6 copy.43
  232.2 2.5 reshape_squeeze.14
  235.1 1.3 copy-done.3
  236.7 2.3 maximum_maximum_fusion
  239.0 46.8 %while.13 = (s32[]{:T(128)}, bf16[4,512,128]{2,1,0:T(8,128)(2,1)}, s32[1]{0:T(128)}, s32[4]{0:T(128)S(1)}, bf16[2,1024,128]{2,1,0:T(8,128)(2,1)}, /*index=5*/bf1...) while((s32[]{:T(128)}, bf16[4,512,128]{2,1,0:T(8,128)(2,1)}, ...), condition=%wide.region_8.9_spmd.clone, body=%wide.region_5.8_spmd.clone.sunk | while | flops 1374293504 | bytes 46968904 | solution.py:127
  239.0 0.7 dynamic_slice.87
  242.9 2.9 fusion.68
  245.8 2.5 fusion.69
  248.3 2.4 fusion.70
  250.7 0.7 dynamic_slice.87
  254.6 2.9 fusion.68
  257.5 2.5 fusion.69
  260.0 2.4 fusion.70
  262.4 0.7 dynamic_slice.87
  266.3 2.9 fusion.68
  269.2 2.5 fusion.69
  271.7 2.4 fusion.70
  278.0 2.9 fusion.68
  280.9 2.5 fusion.69
  283.4 2.4 fusion.70
  285.8 1.2 copy.45
  287.1 4.6 convolution_convert_fusion
  291.7 163.8 %all-gather.3.cloned.1.call-done = bf16[8192,2048]{1,0:T(8,128)(2,1)} async-done(((bf16[1024,2048]{1,0:T(8,128)(2,1)}), bf16[8192,2048]{1,0:T(8,128)(2,1)}) %all-gather.3.cloned.1.call-update) | async-done | bytes 33554448 | tf_op jit(solution)/shard_map/all_gather | solution.py:136
  455.5 14.5 %reduce_sum.70 = bf16[1024,2048]{1,0:T(8,128)(2,1)} reduce(bf16[8,1024,2048]{2,1,0:T(8,128)(2,1)} %bitcast.84, bf16[]{:T(256)} %constant.133.clone.1), dimensions={0}, to_apply=%region_9.10 | reduce | flops 14680064 | bytes 37748736 | tf_op jit(solution)/shard_map/reduce_sum | solution.py:137
  470.0 1.9 constant_dynamic-slice_fusion.1
  (66 shorter events, 5.6 us)
Async XLA Ops:
  6.5 26.4 %copy-start = (bf16[2048,3,256]{2,0,1:T(8,128)(2,1)S(1)}, bf16[2048,3,256]{2,0,1:T(8,128)(2,1)}, u32[]{:S(2)}) copy-start(bf16[2048,3,256]{2,0,1:T(8,128)(2,1)} %param.11) | copy-start | bytes 9437188
  15.7 11.9 %copy-start.9 = (s32[32]{0:T(128)S(1)}, s32[32]{0:T(128)}, u32[]{:S(2)}) copy-start(s32[32]{0:T(128)} %param.17) | copy-start | bytes 388
  15.7 12.6 %copy-start.10 = (s32[32]{0:T(128)S(1)}, s32[32]{0:T(128)}, u32[]{:S(2)}) copy-start(s32[32]{0:T(128)} %param.14) | copy-start | bytes 388
  15.7 201.5 %all-to-all-start = ((bf16[32,2,2,128,256]{4,3,2,1,0:T(8,128)(2,1)}), bf16[32,2,2,128,256]{4,3,2,1,0:T(8,128)(2,1)}, u32[]{:S(2)}, u32[]{:S(2)}) async-start(bf16[32,2,2,128,256]{4,3,2,1,0:T(8,128)(2,1)} %bitcast.85), calls=%async_computation | async-start | bytes 16777216 | tf_op jit(solution)/shard_map/all_to_all | solution.py:93
  27.5 428.0 %all-gather.3.cloned.1.call-start = ((), (), s32[]{:S(2)}) async-start(), calls=%async_computation.1 | async-start | bytes 37748736 | tf_op jit(solution)/shard_map/all_gather | solution.py:136
  27.5 4.1 copy-start.2
  37.0 1.7 copy-start.5
  234.7 1.6 copy-start.3
  234.7 1.7 copy-start.6
  234.8 1.8 copy-start.7
  234.8 2.0 copy-start.8
  245.8 2.5 copy-start.4
  257.5 2.5 copy-start.4
  269.2 2.5 copy-start.4
  280.9 2.5 copy-start.4
  455.5 16.4 %copy-start.1 = (bf16[2048,3,256]{2,0,1:T(8,128)(2,1)S(1)}, bf16[2048,3,256]{2,0,1:T(8,128)(2,1)}, u32[]{:S(2)}) copy-start(bf16[2048,3,256]{2,0,1:T(8,128)(2,1)} %param.11) | copy-start | bytes 9437188
Sparse Core Ops, SparseCore 0:
  291.8 163.6 all-gather.2
